TPU v7x, 256 devices: a whole 4x4x8 slice. The times are simulated.
256 devices in a mesh: row: 16 (over x, z_lo, core), col: 16 (over y, z_hi).
Axes of the slice: x: 4, y: 4, z: 8 (z_hi: 4, z_lo: 2; z = z_hi * 2 + z_lo), core: 2. Of those that a mesh axis runs over, the one named last changes fastest.
Arguments:
- ancestor_inverse: bfloat16 [32768, 32768], P('row', 'col'), may hold values from -0.03125 to 0.03125
- panel: bfloat16 [32768, 512], P(('row', 'col')), may hold values from -0.75 to 0.75
- structure: int32 [2, 128], replicated, may hold values 0 or 1
- diag_inverse: float32 [2, 256, 256], replicated, may hold values from -6 to 6
Outputs:
- upper: bfloat16 [32768, 512], P(('row', 'col'))
- diagonal: float32 [2, 256, 256], replicated
All inputs are finite; a program needn't handle non-finite values.
Results may differ from a plain program's by a relative error of at most 0.0014.
Values may be sent and summed in bfloat16 or wider, within the bound.
A program may use at most 64 MiB of HBM per device.

v0:
```python
import jax
import jax.numpy as jnp
from jax import lax
from jax.sharding import PartitionSpec as P


def from_root(block, axis, source):
    block = jnp.where(lax.axis_index(axis) == source, block, jnp.zeros_like(block))
    return lax.psum(block, axis)


def row_keep(begin_row, length, structure, blk_width):
    blocks_all = structure.shape[1]
    indices = begin_row + jnp.arange(length, dtype=jnp.int32)
    owners = indices // blk_width
    onehot = (owners[:, None] == jnp.arange(blocks_all, dtype=jnp.int32)[None, :]).astype(
        jnp.float32
    )
    keeps = jnp.dot(onehot, structure.T.astype(jnp.float32), preferred_element_type=jnp.float32)
    return jnp.repeat(keeps, blk_width, axis=1)


def diag_part(lower, upper_rows, blk_width):
    snodes = upper_rows.shape[1] // blk_width
    lower_f = lower.astype(jnp.float32).reshape(lower.shape[0], snodes, blk_width)
    upper_f = upper_rows.reshape(upper_rows.shape[0], snodes, blk_width)
    return jnp.einsum("mkw,mkv->kwv", lower_f, upper_f, precision=lax.Precision.HIGHEST)


def local(ancestor_inverse, panel, structure, diag_inverse):
    blk_width = diag_inverse.shape[1]
    row_count = lax.axis_size("row")
    col_count = lax.axis_size("col")
    row_index = lax.axis_index("row")
    col_index = lax.axis_index("col")
    piece_rows = panel.shape[0]
    begin_own = (row_index * col_count + col_index) * piece_rows
    keep_own = row_keep(begin_own, piece_rows, structure, blk_width)
    masked = panel * keep_own.astype(jnp.bfloat16)
    row_block = lax.all_gather(masked, "col", axis=0, tiled=True)
    ratio = col_count // row_count
    root_row = col_index // ratio
    col_block = from_root(row_block, "row", root_row)
    partial_rows = -jnp.dot(ancestor_inverse, col_block, preferred_element_type=jnp.float32)
    full_rows = lax.psum(partial_rows, "col")
    own_rows = lax.dynamic_slice_in_dim(full_rows, col_index * piece_rows, piece_rows, 0)
    diag_sum = lax.psum(diag_part(masked, own_rows, blk_width), ("row", "col"))
    upper = (own_rows * keep_own).astype(jnp.bfloat16)
    diagonal = diag_inverse - diag_sum
    return (upper, diagonal)


def solution(mesh):
    return jax.shard_map(
        local,
        mesh=mesh,
        in_specs=(P("row", "col"), P(("row", "col"), None), P(), P()),
        out_specs=(P(("row", "col"), None), P()),
        check_vma=False,
    )
```

profile of v0, /device:TPU:2, one launch (start us, length us, event | category | flops | bytes accessed | tf_op | source)
XLA Modules:
  0.0 704.9 jit_solution(14977769221147062847)
XLA Ops:
  7.2 0.0 all-gather.2.cloned.1.call-start
  7.2 1.0 copy.8
  8.3 0.9 fusion.2
  9.1 0.7 fusion.1
  9.8 0.0 all-gather.2.cloned.1.call-update
  9.9 0.0 all-reduce.4.cloned.1.call-start
  9.9 66.3 %all-gather.2.cloned.1.call-done = bf16[2048,512]{0,1:T(8,128)(2,1)} async-done(((bf16[128,512]{0,1:T(8,128)(2,1)}), bf16[2048,512]{0,1:T(8,128)(2,1)}) %all-gather.2.cloned.1.call-update) | async-done | bytes 2097168 | tf_op jit(solution)/shard_map/all_gather | solution.py:40
  76.2 1.5 broadcast_select_fusion
  77.7 0.0 all-reduce.4.cloned.1.call-update
  77.7 0.0 all-reduce.6.cloned.1.call-start
  77.8 122.7 %all-reduce.4.cloned.1.call-done = bf16[2048,512]{0,1:T(8,128)(2,1)} async-done(((bf16[2048,512]{0,1:T(8,128)(2,1)}), bf16[2048,512]{0,1:T(8,128)(2,1)}) %all-reduce.4.cloned.1.call-update) | async-done | bytes 2097168 | tf_op jit(solution)/shard_map/psum | solution.py:9
  200.5 10.5 %negate_bitcast_fusion = f32[2048,512]{0,1:T(8,128)} fusion(bf16[2048,512]{0,1:T(8,128)(2,1)} %all-reduce.4.cloned.1.call-done, bf16[2048,2048]{1,0:T(8,128)(2,1)} %param.4), kind=kOutput, calls=%fused_computation | convolution fusion | flops 4296015872 | bytes 14680064 | tf_op jit(solution)/shard_map/dot_general | solution.py:44
  211.0 0.0 copy-start
  211.0 0.0 copy-start.1
  211.0 0.0 all-reduce.6.cloned.1.call-update
  211.0 0.0 all-reduce.8.cloned.1.call-start
  211.1 225.6 %all-reduce.6.cloned.1.call-done = f32[2048,512]{0,1:T(8,128)} async-done(((f32[2048,512]{0,1:T(8,128)}), f32[2048,512]{0,1:T(8,128)}) %all-reduce.6.cloned.1.call-update) | async-done | bytes 4194320 | tf_op jit(solution)/shard_map/psum | solution.py:45
  436.7 1.0 fusion
  437.7 0.0 copy-done
  437.7 1.2 fusion.5
  438.9 0.0 all-reduce.8.cloned.1.call-update
  438.9 0.8 copy.10
  439.7 256.8 %all-reduce.8.cloned.1.call-done = f32[2,256,256]{2,1,0:T(8,128)} async-done(((f32[2,256,256]{2,1,0:T(8,128)}), f32[2,256,256]{2,1,0:T(8,128)}) %all-reduce.8.cloned.1.call-update) | async-done | bytes 524304 | tf_op jit(solution)/shard_map/psum | solution.py:47
  696.4 0.0 copy-done.1
  696.4 1.9 sub.12
  (1 shorter events, 0.0 us)
Async XLA Ops:
  7.2 69.0 %all-gather.2.cloned.1.call-start = ((), (), s32[]{:S(2)}) async-start(), calls=%async_computation | async-start | bytes 2228224 | tf_op jit(solution)/shard_map/all_gather | solution.py:40
  9.9 190.6 %all-reduce.4.cloned.1.call-start = ((), (), s32[]{:S(2)}) async-start(), calls=%async_computation.1 | async-start | bytes 4194304 | tf_op jit(solution)/shard_map/psum | solution.py:9
  77.7 359.0 %all-reduce.6.cloned.1.call-start = ((), (), s32[]{:S(2)}) async-start(), calls=%async_computation.2 | async-start | bytes 8388608 | tf_op jit(solution)/shard_map/psum | solution.py:45
  211.0 226.7 %copy-start = (bf16[128,512]{0,1:T(8,128)(2,1)S(1)}, bf16[128,512]{0,1:T(8,128)(2,1)}, u32[]{:S(2)}) copy-start(bf16[128,512]{0,1:T(8,128)(2,1)} %fusion.1) | copy-start | bytes 393220
  211.0 485.5 %copy-start.1 = (f32[2,256,256]{2,1,0:T(8,128)S(1)}, f32[2,256,256]{2,1,0:T(8,128)}, u32[]{:S(2)}) copy-start(f32[2,256,256]{2,1,0:T(8,128)} %param.7) | copy-start | bytes 1572868
  211.0 485.4 %all-reduce.8.cloned.1.call-start = ((), (), s32[]{:S(2)}) async-start(), calls=%async_computation.3 | async-start | bytes 1048576 | tf_op jit(solution)/shard_map/psum | solution.py:47
Sparse Core Ops, SparseCore 0:
  10.9 65.2 all-gather.1
  78.9 121.5 all-reduce.3
  211.1 225.5 all-reduce.5
  442.6 253.8 all-reduce.7
where the time goes:
time: 705 us
  waiting for transfers between devices  671 us (95%)
  between operations  13.8 us (2%)
  matrix products  12.6 us (2%)
    psum x1, waiting for transfers between devices, local(): diag_sum = lax.psum(diag_part(masked, own_rows, blk_width), ('row', 'col'))  257 us
    psum x1, waiting for transfers between devices, local(): full_rows = lax.psum(partial_rows, 'col')  226 us
    psum x1, waiting for transfers between devices, from_root(): return lax.psum(block, axis)  123 us
    all_gather x1, waiting for transfers between devices, local(): row_block = lax.all_gather(masked, 'col', axis=0, tiled=True)  66.3 us
  transfers between devices with their start and end apart: 4, of which 4 were waited for; matrix products, arithmetic and copies ran while one was open for 0% of the time, Pallas kernels for 0%

commit v1 on v0

--- a/solution.py
+++ b/solution.py
@@ -44,7 +44,8 @@
     partial_rows = -jnp.dot(ancestor_inverse, col_block, preferred_element_type=jnp.float32)
     full_rows = lax.psum(partial_rows, "col")
     own_rows = lax.dynamic_slice_in_dim(full_rows, col_index * piece_rows, piece_rows, 0)
-    diag_sum = lax.psum(diag_part(masked, own_rows, blk_width), ("row", "col"))
+    inner = lax.psum(diag_part(masked, own_rows, blk_width), "row")
+    diag_sum = lax.psum(inner, "col")
     upper = (own_rows * keep_own).astype(jnp.bfloat16)
     diagonal = diag_inverse - diag_sum
     return (upper, diagonal)

time: 705 us -> 741 us (1.051)
  waiting for transfers between devices: 671 us -> 708 us
    psum x1 -> x2, waiting for transfers between devices: 257 us -> 293 us  [the longest x1 176 us: local(): diag_sum = lax.psum(inner, 'col')]
  transfers between devices with their start and end apart: 4 -> 5, of which waited for: 4 -> 5; matrix products, arithmetic and copies ran while one was open for 0% -> 0% of each run, Pallas kernels for 0% -> 0%
where the time goes in v1:
time: 741 us
  waiting for transfers between devices  708 us (96%)
  between operations  13.8 us (2%)
  matrix products  12.6 us (2%)
    psum x1, waiting for transfers between devices, local(): full_rows = lax.psum(partial_rows, 'col')  226 us
    psum x1, waiting for transfers between devices, local(): diag_sum = lax.psum(inner, 'col')  176 us
    psum x1, waiting for transfers between devices, from_root(): return lax.psum(block, axis)  123 us
    psum x1, waiting for transfers between devices, local(): inner = lax.psum(diag_part(masked, own_rows, blk_width), 'row')  117 us
    all_gather x1, waiting for transfers between devices, local(): row_block = lax.all_gather(masked, 'col', axis=0, tiled=True)  66.3 us
  transfers between devices with their start and end apart: 5, of which 5 were waited for; matrix products, arithmetic and copies ran while one was open for 0% of the time, Pallas kernels for 0%

profile of v1, /device:TPU:2, one launch (start us, length us, event | category | flops | bytes accessed | tf_op | source)
XLA Modules:
  0.0 741.0 jit_solution(13015117990419252098)
XLA Ops:
  7.2 0.0 all-gather.2.cloned.1.call-start
  7.2 1.0 copy.8
  8.3 0.9 fusion.2
  9.1 0.7 fusion.1
  9.8 0.0 all-gather.2.cloned.1.call-update
  9.9 0.0 all-reduce.5.cloned.1.call-start
  9.9 66.3 %all-gather.2.cloned.1.call-done = bf16[2048,512]{0,1:T(8,128)(2,1)} async-done(((bf16[128,512]{0,1:T(8,128)(2,1)}), bf16[2048,512]{0,1:T(8,128)(2,1)}) %all-gather.2.cloned.1.call-update) | async-done | bytes 2097168 | tf_op jit(solution)/shard_map/all_gather | solution.py:40
  76.2 1.5 broadcast_select_fusion
  77.7 0.0 all-reduce.5.cloned.1.call-update
  77.7 0.0 all-reduce.7.cloned.1.call-start
  77.8 122.7 %all-reduce.5.cloned.1.call-done = bf16[2048,512]{0,1:T(8,128)(2,1)} async-done(((bf16[2048,512]{0,1:T(8,128)(2,1)}), bf16[2048,512]{0,1:T(8,128)(2,1)}) %all-reduce.5.cloned.1.call-update) | async-done | bytes 2097168 | tf_op jit(solution)/shard_map/psum | solution.py:9
  200.5 10.5 %negate_bitcast_fusion = f32[2048,512]{0,1:T(8,128)} fusion(bf16[2048,512]{0,1:T(8,128)(2,1)} %all-reduce.5.cloned.1.call-done, bf16[2048,2048]{1,0:T(8,128)(2,1)} %param.4), kind=kOutput, calls=%fused_computation | convolution fusion | flops 4296015872 | bytes 14680064 | tf_op jit(solution)/shard_map/dot_general | solution.py:44
  211.0 0.0 copy-start
  211.0 0.0 copy-start.1
  211.0 0.0 all-reduce.7.cloned.1.call-update
  211.0 0.0 all-reduce.9.cloned.1.call-start
  211.1 225.6 %all-reduce.7.cloned.1.call-done = f32[2048,512]{0,1:T(8,128)} async-done(((f32[2048,512]{0,1:T(8,128)}), f32[2048,512]{0,1:T(8,128)}) %all-reduce.7.cloned.1.call-update) | async-done | bytes 4194320 | tf_op jit(solution)/shard_map/psum | solution.py:45
  436.7 1.0 fusion
  437.7 0.0 copy-done
  437.7 1.2 fusion.5
  438.9 0.0 all-reduce.9.cloned.1.call-update
  438.9 0.0 all-reduce.11.cloned.1.call-start
  438.9 117.3 %all-reduce.9.cloned.1.call-done = f32[2,256,256]{2,1,0:T(8,128)} async-done(((f32[2,256,256]{2,1,0:T(8,128)}), f32[2,256,256]{2,1,0:T(8,128)}) %all-reduce.9.cloned.1.call-update) | async-done | bytes 524304 | tf_op jit(solution)/shard_map/psum | solution.py:47
  556.3 0.0 all-reduce.11.cloned.1.call-update
  556.3 0.8 copy.10
  557.1 175.5 %all-reduce.11.cloned.1.call-done = f32[2,256,256]{2,1,0:T(8,128)} async-done(((f32[2,256,256]{2,1,0:T(8,128)}), f32[2,256,256]{2,1,0:T(8,128)}) %all-reduce.11.cloned.1.call-update) | async-done | bytes 524304 | tf_op jit(solution)/shard_map/psum | solution.py:48
  732.6 0.0 copy-done.1
  732.6 1.9 sub.12
  (1 shorter events, 0.0 us)
Async XLA Ops:
  7.2 69.0 %all-gather.2.cloned.1.call-start = ((), (), s32[]{:S(2)}) async-start(), calls=%async_computation | async-start | bytes 2228224 | tf_op jit(solution)/shard_map/all_gather | solution.py:40
  9.9 190.6 %all-reduce.5.cloned.1.call-start = ((), (), s32[]{:S(2)}) async-start(), calls=%async_computation.1 | async-start | bytes 4194304 | tf_op jit(solution)/shard_map/psum | solution.py:9
  77.7 359.0 %all-reduce.7.cloned.1.call-start = ((), (), s32[]{:S(2)}) async-start(), calls=%async_computation.2 | async-start | bytes 8388608 | tf_op jit(solution)/shard_map/psum | solution.py:45
  211.0 226.7 %copy-start = (bf16[128,512]{0,1:T(8,128)(2,1)S(1)}, bf16[128,512]{0,1:T(8,128)(2,1)}, u32[]{:S(2)}) copy-start(bf16[128,512]{0,1:T(8,128)(2,1)} %fusion.1) | copy-start | bytes 393220
  211.0 521.6 %copy-start.1 = (f32[2,256,256]{2,1,0:T(8,128)S(1)}, f32[2,256,256]{2,1,0:T(8,128)}, u32[]{:S(2)}) copy-start(f32[2,256,256]{2,1,0:T(8,128)} %param.7) | copy-start | bytes 1572868
  211.0 345.3 %all-reduce.9.cloned.1.call-start = ((), (), s32[]{:S(2)}) async-start(), calls=%async_computation.3 | async-start | bytes 1048576 | tf_op jit(solution)/shard_map/psum | solution.py:47
  438.9 293.7 %all-reduce.11.cloned.1.call-start = ((), (), s32[]{:S(2)}) async-start(), calls=%async_computation.4 | async-start | bytes 1048576 | tf_op jit(solution)/shard_map/psum | solution.py:48
Sparse Core Ops, SparseCore 0:
  10.9 65.2 all-gather.1
  78.9 121.5 all-reduce.4
  211.1 225.5 all-reduce.6
  439.7 116.5 all-reduce.8
  558.8 173.7 all-reduce.10
